TPU v7x, 256 devices: a whole 4x4x8 slice. The times are simulated.
256 devices in a mesh: gz: 64 (over x, y, z_lo, core), gy: 4 (over z_hi).
Axes of the slice: x: 4, y: 4, z: 8 (z_hi: 4, z_lo: 2; z = z_hi * 2 + z_lo), core: 2. Of those that a mesh axis runs over, the one named last changes fastest.
Arguments:
- coarse_six: float32 [512, 1024, 512], P('gz', 'gy'), may hold values from 0.1 to 10
Outputs:
- detail_seven: float32 [512, 1024, 512], P('gz', 'gy')
- coarse_seven: float32 [512, 1024, 512], P('gz', 'gy')
All inputs are finite; a program needn't handle non-finite values.
Results may differ from a plain program's by a relative error of at most 0.00002.
Values sent between devices are 32-bit elements; how exact they have to be, the bound alone decides.
A program may use at most 128 MiB of HBM per device.

v0:
```python
import jax
import jax.numpy as jnp
from jax import lax
from jax.sharding import PartitionSpec as P

TAP_DILATION = 32


kernel_weights = (0.0625, 0.25, 0.375, 0.25, 0.0625)


def passed_along(x, axis, by):
    peers = lax.axis_size(axis)
    return lax.ppermute(x, axis, [(i, (i + by) % peers) for i in range(peers)])


def with_halo(x, sides, width):
    for axis, dim in sides:
        peers, length = (lax.axis_size(axis), x.shape[dim])
        up = [(i, (i + 1) % peers) for i in range(peers)]
        down = [(j, i) for i, j in up]
        last = lax.slice_in_dim(x, length - width, length, axis=dim)
        leading = lax.slice_in_dim(x, 0, width, axis=dim)
        before = lax.ppermute(last, axis, up)
        after = lax.ppermute(leading, axis, down)
        x = jnp.concatenate([before, x, after], axis=dim)
    return x


def smooth_axis(density_field, axis_ordinal):
    weighted_total = jnp.zeros_like(density_field)
    for cell_position in range(5):
        weighted_total = weighted_total + kernel_weights[cell_position] * jnp.roll(
            density_field, -(cell_position - 2) * TAP_DILATION, axis=axis_ordinal
        )
    return weighted_total


def window_sum(extended, length, axis_ordinal):
    weighted_total = None
    for cell_position in range(5):
        start_index = cell_position * TAP_DILATION
        piece = lax.slice_in_dim(extended, start_index, start_index + length, axis=axis_ordinal)
        term = kernel_weights[cell_position] * piece
        weighted_total = term if weighted_total is None else weighted_total + term
    return weighted_total


def z_plane_smooth(density_field):
    count = lax.axis_size("gz")
    plane_stack = density_field.shape[0]
    weighted_total = kernel_weights[2] * density_field
    for cell_position in (0, 1, 3, 4):
        filter_reach = (cell_position - 2) * TAP_DILATION // plane_stack
        moved = -filter_reach % count
        fetched = passed_along(density_field, "gz", moved)
        weighted_total = weighted_total + kernel_weights[cell_position] * fetched
    return weighted_total


def shards(coarse_six):
    along_z = z_plane_smooth(coarse_six)
    local_rows = along_z.shape[1]
    extended = with_halo(along_z, (("gy", 1),), 2 * TAP_DILATION)
    along_y = window_sum(extended, local_rows, 1)
    coarse_seven = smooth_axis(along_y, 2)
    return (coarse_six - coarse_seven, coarse_seven)


def solution(mesh):
    return jax.shard_map(
        shards,
        mesh=mesh,
        in_specs=(P("gz", "gy", None),),
        out_specs=(P("gz", "gy", None), P("gz", "gy", None)),
        check_vma=False,
    )
```

profile of v0, /device:TPU:64, one launch (start us, length us, event | category | flops | bytes accessed | tf_op | source)
XLA Modules:
  0.0 366.9 jit_solution(17140089492029250271)
XLA Ops:
  0.6 5.3 %collective-permute-start.2 = (f32[8,256,512]{2,1,0:T(8,128)}, f32[8,256,512]{2,1,0:T(8,128)S(1)}, u32[]{:S(2)}, u32[]{:S(2)}) collective-permute-start(f32[8,256,512]{2,1,0:T(8,128)} %param.1), channel_id=1, source_target_pairs={{0,240},{4,244},{8,248},{12,252},{16,0},{20,4},{24,8},{28,12},{32,... | collective-permute-start | bytes 12582920 | tf_op jit(solution)/shard_map/ppermute | solution.py:14
  5.9 0.0 collective-permute-start.1
  5.9 0.0 collective-permute-start
  5.9 5.6 %collective-permute-start.3 = (f32[8,256,512]{2,1,0:T(8,128)}, f32[8,256,512]{2,1,0:T(8,128)}, u32[]{:S(2)}, u32[]{:S(2)}) collective-permute-start(f32[8,256,512]{2,1,0:T(8,128)} %param.1), channel_id=1, source_target_pairs={{0,224},{4,228},{8,232},{12,236},{16,240},{20,244},{24,248},{28,25... | collective-permute-start | bytes 12582920 | tf_op jit(solution)/shard_map/ppermute | solution.py:14
  11.6 172.7 %collective-permute-done.2 = f32[8,256,512]{2,1,0:T(8,128)S(1)} collective-permute-done((f32[8,256,512]{2,1,0:T(8,128)}, f32[8,256,512]{2,1,0:T(8,128)S(1)}, u32[]{:S(2)}, u32[]{:S(2)}) %collective-permute-start.2) | collective-permute-done | bytes 4194336 | tf_op jit(solution)/shard_map/ppermute | solution.py:14
  184.3 0.0 copy-start.1
  184.3 4.4 %collective-permute-done.1 = f32[8,256,512]{2,1,0:T(8,128)S(1)} collective-permute-done((f32[8,256,512]{2,1,0:T(8,128)}, f32[8,256,512]{2,1,0:T(8,128)S(1)}, u32[]{:S(2)}, u32[]{:S(2)}) %collective-permute-start.1) | collective-permute-done | bytes 4194336 | tf_op jit(solution)/shard_map/ppermute | solution.py:14
  188.6 0.0 copy-start.2
  188.6 87.3 %collective-permute-done = f32[8,256,512]{2,1,0:T(8,128)S(1)} collective-permute-done((f32[8,256,512]{2,1,0:T(8,128)}, f32[8,256,512]{2,1,0:T(8,128)S(1)}, u32[]{:S(2)}, u32[]{:S(2)}) %collective-permute-start) | collective-permute-done | bytes 4194336 | tf_op jit(solution)/shard_map/ppermute | solution.py:14
  275.9 0.0 copy-done.1
  275.9 0.0 copy-done.2
  275.9 0.0 copy-start.3
  275.9 2.0 copy-done.3
  277.9 4.9 %collective-permute-done.3 = f32[8,256,512]{2,1,0:T(8,128)} collective-permute-done((f32[8,256,512]{2,1,0:T(8,128)}, f32[8,256,512]{2,1,0:T(8,128)}, u32[]{:S(2)}, u32[]{:S(2)}) %collective-permute-start.3) | collective-permute-done | bytes 4194336 | tf_op jit(solution)/shard_map/ppermute | solution.py:14
  282.8 9.7 %multiply_add_fusion = f32[8,256,512]{2,1,0:T(8,128)S(1)} fusion(f32[8,256,512]{2,1,0:T(8,128)} %collective-permute-done.3, f32[8,256,512]{2,1,0:T(8,128)} %copy-done.1, f32[8,256,512]{2,1,0:T(8,128)} %copy-done.2, f32[8,256,512]{2,1,0:T(8,128)} %copy-done.3, f32[8,256,512]{2,1,0:T(8,128)} %param.1), kind=kLoop, calls=%fused_computation.24 | loop fusion | flops 9437184 | bytes 25165824 | tf_op jit(solution)/shard_map/add | solution.py:57
  292.5 0.2 fusion.20
  292.7 4.6 %collective-permute-start.4 = (f32[8,64,512]{2,1,0:T(8,128)S(1)}, f32[8,64,512]{2,1,0:T(8,128)S(1)}, u32[]{:S(2)}, u32[]{:S(2)}) collective-permute-start(f32[8,64,512]{2,1,0:T(8,128)S(1)} %get-tuple-element.12), channel_id=1, source_target_pairs={{0,1},{1,2},{2,3},{3,0},{4,5},{5,6},{6,7},{7,4},{8,9},{9,10},{10,1... | collective-permute-start | bytes 3145736 | tf_op jit(solution)/shard_map/ppermute | solution.py:24
  297.2 0.0 collective-permute-start.5
  297.3 43.6 %collective-permute-done.4 = f32[8,64,512]{2,1,0:T(8,128)S(1)} collective-permute-done((f32[8,64,512]{2,1,0:T(8,128)S(1)}, f32[8,64,512]{2,1,0:T(8,128)S(1)}, u32[]{:S(2)}, u32[]{:S(2)}) %collective-permute-start.4) | collective-permute-done | bytes 1048608 | tf_op jit(solution)/shard_map/ppermute | solution.py:24
  340.9 4.3 %collective-permute-done.5 = f32[8,64,512]{2,1,0:T(8,128)S(1)} collective-permute-done((f32[8,64,512]{2,1,0:T(8,128)S(1)}, f32[8,64,512]{2,1,0:T(8,128)S(1)}, u32[]{:S(2)}, u32[]{:S(2)}) %collective-permute-start.5) | collective-permute-done | bytes 1048608 | tf_op jit(solution)/shard_map/ppermute | solution.py:25
  345.2 2.7 fusion.3
  347.8 0.4 fusion.18
  348.2 1.4 fusion.16
  349.7 3.6 fusion.19
  353.3 0.0 copy-start
  353.3 4.7 %fusion.17 = (f32[8,256,448]{2,1,0:T(8,128)}, f32[8,256,448]{2,1,0:T(8,128)}) fusion(f32[8,256,512]{2,1,0:T(8,128)S(1)} %fusion.3), kind=kLoop, calls=%fused_computation.27 | loop fusion | bytes 14680064 | tf_op jit(solution)/shard_map/jit(_roll_static)/slice | solution.py:33
  358.0 0.0 copy-done
  358.0 8.9 %fusion.14 = (f32[8,256,512]{2,1,0:T(8,128)}, f32[8,256,512]{2,1,0:T(8,128)}) fusion(f32[8,256,512]{2,1,0:T(8,128)S(1)} %copy-done, f32[8,256,64]{2,1,0:T(8,128)} %get-tuple-element.5, f32[8,256,448]{2,1,0:T(8,128)} %get-tuple-element.7, f32[8,256,32]{2,1,0:T(8,128)S(1)} %get-tuple-element.9, f32[8,256,480]{2,1,0:T(8,128)} %get-tuple-element.11, ...), kind=kLoop, calls=%fused_computation.25 | loop fusion | flops 14680064 | bytes 33554432 | tf_op jit(solution)/shard_map/sub | solution.py:67
Async XLA Ops:
  0.6 183.6 %collective-permute-start.2 = (f32[8,256,512]{2,1,0:T(8,128)}, f32[8,256,512]{2,1,0:T(8,128)S(1)}, u32[]{:S(2)}, u32[]{:S(2)}) collective-permute-start(f32[8,256,512]{2,1,0:T(8,128)} %param.1), channel_id=1, source_target_pairs={{0,240},{4,244},{8,248},{12,252},{16,0},{20,4},{24,8},{28,12},{32,... | collective-permute-start | bytes 12582920 | tf_op jit(solution)/shard_map/ppermute | solution.py:14
  5.9 182.7 %collective-permute-start.1 = (f32[8,256,512]{2,1,0:T(8,128)}, f32[8,256,512]{2,1,0:T(8,128)S(1)}, u32[]{:S(2)}, u32[]{:S(2)}) collective-permute-start(f32[8,256,512]{2,1,0:T(8,128)} %param.1), channel_id=1, source_target_pairs={{0,16},{4,20},{8,24},{12,28},{16,32},{20,36},{24,40},{28,44},{32,4... | collective-permute-start | bytes 12582920 | tf_op jit(solution)/shard_map/ppermute | solution.py:14
  5.9 270.0 %collective-permute-start = (f32[8,256,512]{2,1,0:T(8,128)}, f32[8,256,512]{2,1,0:T(8,128)S(1)}, u32[]{:S(2)}, u32[]{:S(2)}) collective-permute-start(f32[8,256,512]{2,1,0:T(8,128)} %param.1), channel_id=1, source_target_pairs={{0,32},{4,36},{8,40},{12,44},{16,48},{20,52},{24,56},{28,60},{32,6... | collective-permute-start | bytes 12582920 | tf_op jit(solution)/shard_map/ppermute | solution.py:14
  5.9 276.8 %collective-permute-start.3 = (f32[8,256,512]{2,1,0:T(8,128)}, f32[8,256,512]{2,1,0:T(8,128)}, u32[]{:S(2)}, u32[]{:S(2)}) collective-permute-start(f32[8,256,512]{2,1,0:T(8,128)} %param.1), channel_id=1, source_target_pairs={{0,224},{4,228},{8,232},{12,236},{16,240},{20,244},{24,248},{28,25... | collective-permute-start | bytes 12582920 | tf_op jit(solution)/shard_map/ppermute | solution.py:14
  184.3 91.6 %copy-start.1 = (f32[8,256,512]{2,1,0:T(8,128)}, f32[8,256,512]{2,1,0:T(8,128)S(1)}, u32[]{:S(2)}) copy-start(f32[8,256,512]{2,1,0:T(8,128)S(1)} %collective-permute-done.2) | copy-start | bytes 12582916
  188.6 87.3 %copy-start.2 = (f32[8,256,512]{2,1,0:T(8,128)}, f32[8,256,512]{2,1,0:T(8,128)S(1)}, u32[]{:S(2)}) copy-start(f32[8,256,512]{2,1,0:T(8,128)S(1)} %collective-permute-done.1) | copy-start | bytes 12582916
  275.9 2.0 copy-start.3
  292.7 48.2 %collective-permute-start.4 = (f32[8,64,512]{2,1,0:T(8,128)S(1)}, f32[8,64,512]{2,1,0:T(8,128)S(1)}, u32[]{:S(2)}, u32[]{:S(2)}) collective-permute-start(f32[8,64,512]{2,1,0:T(8,128)S(1)} %get-tuple-element.12), channel_id=1, source_target_pairs={{0,1},{1,2},{2,3},{3,0},{4,5},{5,6},{6,7},{7,4},{8,9},{9,10},{10,1... | collective-permute-start | bytes 3145736 | tf_op jit(solution)/shard_map/ppermute | solution.py:24
  297.2 47.9 %collective-permute-start.5 = (f32[8,64,512]{2,1,0:T(8,128)S(1)}, f32[8,64,512]{2,1,0:T(8,128)S(1)}, u32[]{:S(2)}, u32[]{:S(2)}) collective-permute-start(f32[8,64,512]{2,1,0:T(8,128)S(1)} %get-tuple-element.13), channel_id=1, source_target_pairs={{1,0},{2,1},{3,2},{0,3},{5,4},{6,5},{7,6},{4,7},{9,8},{10,9},{11,1... | collective-permute-start | bytes 3145736 | tf_op jit(solution)/shard_map/ppermute | solution.py:25
  353.3 4.7 %copy-start = (f32[8,256,512]{2,1,0:T(8,128)S(1)}, f32[8,256,512]{2,1,0:T(8,128)}, u32[]{:S(2)}) copy-start(f32[8,256,512]{2,1,0:T(8,128)} %param.1) | copy-start | bytes 12582916
where the time goes:
time: 367 us
  waiting for transfers between devices  317 us (86%)
  other arithmetic  21.2 us (6%)
  starting transfers between devices  15.5 us (4%)
  local copies, waits for them, and re-layouts  12.3 us (3%)
    ppermute x4, waiting for transfers between devices, passed_along(): return lax.ppermute(x, axis, [(i, (i + by) % peers) for i in range(peers)])  269 us
    ppermute x1, waiting for transfers between devices, with_halo(): before = lax.ppermute(last, axis, up)  43.6 us
    ppermute x4, starting transfers between devices, passed_along(): return lax.ppermute(x, axis, [(i, (i + by) % peers) for i in range(peers)])  10.9 us
    slice x4, local copies, waits for them, and re-layouts, smooth_axis(): jnp.roll(density_field, -(cell_position - 2) * TAP_DILATION, axis=axis_or...  10.1 us
    add x1, other arithmetic, z_plane_smooth(): weighted_total = weighted_total + kernel_weights[cell_position] * fetched  9.71 us
    sub x1, other arithmetic, shards(): return (coarse_six - coarse_seven, coarse_seven)  8.87 us
  transfers between devices with their start and end apart: 6, of which 6 were waited for; matrix products, arithmetic and copies ran while one was open for 0% of the time, Pallas kernels for 0%

commit v1 on v0

v1 whole, which is shorter than its diff:
```python
import functools

import jax
import jax.numpy as jnp
from jax import lax
from jax.experimental import pallas as pl
from jax.experimental.pallas import tpu as pltpu
from jax.sharding import PartitionSpec as P

MESH = pl.DeviceIdType.MESH
F32 = jnp.float32

PLANES, ROWS, COLS = 8, 256, 512
RING = 16
PIECE = ROWS // RING
DIL = 32
HALO = 2 * DIL
EARLY = 2
SCALE = 1.0 / 4096.0
HOPS = tuple((a, b) for a in range(4) for b in range(4) if a or b)


def place():
    g, h = lax.axis_index("gz"), lax.axis_index("gy")
    return g // 16, (g // 4) % 4, g % 4, h


def device(dx, dy):
    x, y, r, h = place()
    return (((x + dx) % 4) * 16 + ((y + dy) % 4) * 4 + r, h)


def ring_index(dx, dy):
    x, y, _, _ = place()
    return ((x + dx) % 4) * 4 + (y + dy) % 4


def gy_device(dh):
    g, h = lax.axis_index("gz"), lax.axis_index("gy")
    return (g, (h + dh) % 4)


def smooth_x(src, dst, j):
    lane = lax.broadcasted_iota(jnp.int32, (8, 128), 1)
    low, high = lane < 96, lane >= 32

    def row_tile(t):
        rows = pl.ds(pl.multiple_of(t * 8, 8), 8)
        v = [src[j, rows, 128 * k : 128 * k + 128] for k in range(4)]
        for _ in range(2):
            r = [pltpu.roll(a, 96, 1) for a in v]
            v = [v[k] + jnp.where(low, r[k], r[(k + 1) % 4]) for k in range(4)]
            r = [pltpu.roll(a, 32, 1) for a in v]
            v = [v[k] + jnp.where(high, r[k], r[(k + 3) % 4]) for k in range(4)]
        for k in range(4):
            dst[j, rows, 128 * k : 128 * k + 128] = v[k]

    @pl.loop(0, ROWS // 32)
    def _(t):
        for u in range(4):
            row_tile(t * 4 + u)


def smooth_y(src, before, after, j, emit):
    @pl.loop(0, DIL // 8)
    def _(t):
        for k in range(4):
            cols = slice(128 * k, 128 * k + 128)

            def at(ref, start):
                return ref[j, pl.ds(pl.multiple_of(start + t * 8, 8), 8), cols]

            v = [at(before, 0), at(before, DIL)]
            v += [at(src, DIL * i) for i in range(ROWS // DIL)]
            v += [at(after, 0), at(after, DIL)]
            for _ in range(4):
                v = [v[i] + v[i + 1] for i in range(len(v) - 1)]
            for i in range(ROWS // DIL):
                emit(pl.ds(pl.multiple_of(DIL * i + t * 8, 8), 8), cols, v[i])


def smooth_z(src, dst, j):
    for t in range(PIECE // 8):
        for k in range(4):
            rows, cols = slice(8 * t, 8 * t + 8), slice(128 * k, 128 * k + 128)
            v = [src[j, q, rows, cols] for q in range(RING)]
            for _ in range(4):
                v = [v[q] + v[(q + 1) % RING] for q in range(RING)]
            for q in range(RING):
                dst[j, q, rows, cols] = v[(q - 2) % RING] * SCALE


def kernel(x_ref, detail_ref, coarse_ref, xin, xs, ys, gathered, smoothed, back, before, after, detail,
           load_sem, f_send, f_recv, b_send, b_recv, h_send, h_recv, o_sem):
    me = ring_index(0, 0)

    def load(j):
        return pltpu.make_async_copy(x_ref.at[j], xin.at[j], load_sem.at[j])

    def forth(j, src, k):
        dx, dy = HOPS[k]
        rows = pl.ds(pl.multiple_of(ring_index(dx, dy) * PIECE, PIECE), PIECE)
        return pltpu.make_async_remote_copy(
            src.at[j, rows], gathered.at[j, me], f_send.at[j, k], f_recv.at[j, k],
            device_id=device(dx, dy), device_id_type=MESH)

    def home(j, k):
        dx, dy = HOPS[k]
        rows = pl.ds(pl.multiple_of(me * PIECE, PIECE), PIECE)
        return pltpu.make_async_remote_copy(
            smoothed.at[j, ring_index(dx, dy)], back.at[j, rows], b_send.at[j, k], b_recv.at[j, k],
            device_id=device(dx, dy), device_id_type=MESH)

    def halo(j, src, side):
        if side == 0:
            return pltpu.make_async_remote_copy(
                src.at[j, pl.ds(ROWS - HALO, HALO)], before.at[j], h_send.at[j, 0], h_recv.at[j, 0],
                device_id=gy_device(1), device_id_type=MESH)
        return pltpu.make_async_remote_copy(
            src.at[j, pl.ds(0, HALO)], after.at[j], h_send.at[j, 1], h_recv.at[j, 1],
            device_id=gy_device(3), device_id_type=MESH)

    def store(j, which):
        src, dst = ((detail, detail_ref), (back, coarse_ref))[which]
        return pltpu.make_async_copy(src.at[j], dst.at[j], o_sem.at[j, which])

    mine = pl.ds(pl.multiple_of(me * PIECE, PIECE), PIECE)

    def send_forth(j, src):
        for k in range(len(HOPS)):
            forth(j, src, k).start()
        gathered[j, me] = src[j, mine]

    def step_z(j):
        for k in range(len(HOPS)):
            forth(j, xs, k).wait_recv()
        smooth_z(gathered, smoothed, j)
        for k in range(len(HOPS)):
            home(j, k).start()
        back[j, mine] = smoothed[j, me]

    def step_y(j):
        for side in range(2):
            halo(j, xs, side).wait_recv()

        def emit(rows, cols, value):
            ys[j, rows, cols] = value

        smooth_y(xs, before, after, j, emit)
        send_forth(j, ys)

    def finish(j):
        @pl.loop(0, ROWS // 32)
        def _(t):
            rows = pl.ds(pl.multiple_of(t * 32, 32), 32)
            detail[j, rows] = xin[j, rows] - back[j, rows]

        store(j, 0).start()
        store(j, 1).start()

    for j in range(PLANES):
        load(j).start()
    barrier = pltpu.get_barrier_semaphore()
    for dx, dy in HOPS:
        pl.semaphore_signal(barrier, inc=1, device_id=device(dx, dy), device_id_type=MESH)
    for dh in (1, 3):
        pl.semaphore_signal(barrier, inc=1, device_id=gy_device(dh), device_id_type=MESH)
    load(0).wait()
    smooth_x(xin, xs, 0)
    pl.semaphore_wait(barrier, len(HOPS) + 2)
    send_forth(0, xs)

    @pl.loop(1, EARLY)
    def _(j):
        load(j).wait()
        smooth_x(xin, xs, j)
        send_forth(j, xs)

    @pl.loop(EARLY, PLANES)
    def _(j):
        load(j).wait()
        smooth_x(xin, xs, j)
        for side in range(2):
            halo(j, xs, side).start()

    @pl.loop(0, PLANES)
    def _(i):
        @pl.when(i < PLANES - EARLY)
        def _():
            step_y(i + EARLY)

        step_z(i)

        @pl.when((i >= 3) & (i < 3 + EARLY))
        def _():
            j = i - 3
            for k in range(len(HOPS)):
                home(j, k).wait_recv()
            for side in range(2):
                halo(j, back, side).start()

    @pl.loop(0, EARLY)
    def _(j):
        for side in range(2):
            halo(j, back, side).wait()

        def emit(rows, cols, value):
            ys[j, rows, cols] = value

        smooth_y(back, before, after, j, emit)

        @pl.loop(0, ROWS // 32)
        def _(t):
            rows = pl.ds(pl.multiple_of(t * 32, 32), 32)
            back[j, rows] = ys[j, rows]

        finish(j)

    @pl.loop(EARLY, PLANES)
    def _(j):
        for k in range(len(HOPS)):
            home(j, k).wait_recv()
        finish(j)

    @pl.loop(EARLY, PLANES)
    def _(j):
        for side in range(2):
            halo(j, xs, side).wait_send()

    @pl.loop(0, PLANES)
    def _(j):
        for k in range(len(HOPS)):
            forth(j, xs, k).wait_send()
            home(j, k).wait_send()
        store(j, 0).wait()
        store(j, 1).wait()


def shards(coarse_six):
    block = jax.ShapeDtypeStruct((PLANES, ROWS, COLS), F32)
    full = pltpu.VMEM((PLANES, ROWS, COLS), F32)
    pieces = pltpu.VMEM((PLANES, RING, PIECE, COLS), F32)
    edge = pltpu.VMEM((PLANES, HALO, COLS), F32)
    dma = pltpu.SemaphoreType.DMA
    n = len(HOPS)
    return pl.pallas_call(
        kernel,
        out_shape=(block, block),
        in_specs=[pl.BlockSpec(memory_space=pl.ANY)],
        out_specs=(pl.BlockSpec(memory_space=pl.ANY),) * 2,
        scratch_shapes=[full, full, full, pieces, pieces, full, edge, edge, full,
                        dma((PLANES,)), dma((PLANES, n)), dma((PLANES, n)), dma((PLANES, n)), dma((PLANES, n)),
                        dma((PLANES, 2)), dma((PLANES, 2)), dma((PLANES, 2))],
        compiler_params=pltpu.CompilerParams(collective_id=0, has_side_effects=True, vmem_limit_bytes=44 << 20),
        name="starlet",
    )(coarse_six)


def solution(mesh):
    return jax.shard_map(
        shards,
        mesh=mesh,
        in_specs=(P("gz", "gy", None),),
        out_specs=(P("gz", "gy", None), P("gz", "gy", None)),
        check_vma=False,
    )
```

time: 367 us -> 121 us (0.33)
  the two profiles are of different devices: /device:TPU:64 before, /device:TPU:188 now
where the time goes in v1:
time: 121 us
  Pallas kernels  117 us (97%)
  local copies, waits for them, and re-layouts  4.03 us (3%)
    pallas_call x1, Pallas kernels, shards(): pl.pallas_call(kernel, out_shape=(block, block), in_specs=[pl.BlockSpec(m...  117 us
    unnamed x2, local copies, waits for them, and re-layouts  4.03 us

profile of v1, /device:TPU:188, one launch (start us, length us, event | category | flops | bytes accessed | tf_op | source)
XLA Modules:
  0.0 121.3 jit_solution(17421238710480490276)
XLA Ops:
  0.6 116.7 %starlet.1 = (f32[8,256,512]{2,1,0:T(8,128)S(1)}, f32[8,256,512]{2,1,0:T(8,128)S(1)}) custom-call(f32[8,256,512]{2,1,0:T(8,128)} %x_ref.1), custom_call_target="tpu_custom_call" | custom-call | tf_op jit(solution)/shard_map/starlet/pallas_call | solution.py:246
  117.3 2.0 %copy.5 = f32[8,256,512]{2,1,0:T(8,128)} copy(f32[8,256,512]{2,1,0:T(8,128)S(1)} %get-tuple-element.4) | data formatting | bytes 8388608
  119.3 2.0 %copy.6 = f32[8,256,512]{2,1,0:T(8,128)} copy(f32[8,256,512]{2,1,0:T(8,128)S(1)} %get-tuple-element.5) | data formatting | bytes 8388608

commit v2 on v1

v2 whole, which is shorter than its diff:
```python
import functools

import jax
import jax.numpy as jnp
from jax import lax
from jax.experimental import pallas as pl
from jax.experimental.pallas import tpu as pltpu
from jax.sharding import PartitionSpec as P

MESH = pl.DeviceIdType.MESH
F32 = jnp.float32

PLANES, ROWS, COLS = 8, 256, 512
RING = 4
PIECE = ROWS // RING
TILES = PIECE // 8
SENT = 3 * TILES + TILES - 2
DIL = 32
HALO = 2 * DIL
EARLY = 4
LAGZ, LAG1, LAG2 = 1, 4, 6
SCALE = 1.0 / 4096.0
HOPS = (1, 3, 2)
GREET = ((0, 1), (0, 2), (0, 3), (1, 0), (3, 0))


def place():
    g, h = lax.axis_index("gz"), lax.axis_index("gy")
    return g // 16, (g // 4) % 4, g % 4, h


def device(dx, dy):
    x, y, r, h = place()
    return (((x + dx) % 4) * 16 + ((y + dy) % 4) * 4 + r, h)


def ring_index(dy):
    return (place()[1] + dy) % 4


def gy_device(dh):
    g, h = lax.axis_index("gz"), lax.axis_index("gy")
    return (g, (h + dh) % 4)


def tile(start):
    return pl.ds(pl.multiple_of(start, 8), 8)


def smooth_x(src, j, emit):
    lane = lax.broadcasted_iota(jnp.int32, (8, 128), 1)
    left, low, high = lane < 64, lane < 96, lane >= 32

    @pl.loop(0, ROWS // 32)
    def _(t):
        for u in range(4):
            v = [src[j, tile(t * 32 + 8 * u), 128 * k : 128 * k + 128] for k in range(4)]
            up = [pltpu.roll(a, 96, 1) for a in v]
            half = [pltpu.roll(a, 64, 1) for a in v]
            down = [pltpu.roll(a, 32, 1) for a in v]
            for k in range(4):
                after, before = (k + 1) % 4, (k + 3) % 4
                near = jnp.where(low, up[k], up[after]) + jnp.where(high, down[k], down[before])
                far = half[k] + jnp.where(left, half[before], half[after])
                emit(t, 8 * u, k, 6.0 * v[k] + (4.0 * near + far))


def smooth_y(src, before, after, j, emit):
    @pl.loop(0, DIL // 8)
    def _(t):
        for k in range(4):
            cols = slice(128 * k, 128 * k + 128)

            def at(ref, start):
                return ref[j, tile(start + t * 8), cols]

            v = [at(before, 0), at(before, DIL)]
            v += [at(src, DIL * i) for i in range(ROWS // DIL)]
            v += [at(after, 0), at(after, DIL)]
            for _ in range(4):
                v = [v[i] + v[i + 1] for i in range(len(v) - 1)]
            for i in range(ROWS // DIL):
                emit(i, t * 8, k, v[i])


def pack_last(column, dst, j):
    low = lax.broadcasted_iota(jnp.int32, (8, 128), 1) < 96
    for p in range(RING):
        v = [column[PIECE * p + 8 * t : PIECE * p + 8 * t + 8, :] for t in range(TILES)]
        for t in range(TILES - 2):
            moved = pltpu.roll(v[TILES - 2 + t // 3], 96 - 32 * (t % 3), 1)
            dst[j, p, 8 * (3 * TILES + t) : 8 * (3 * TILES + t) + 8, :] = jnp.where(low, v[t], moved)


def unpack(src, j, emit):
    lane = lax.broadcasted_iota(jnp.int32, (8, 128), 1)
    low, one, two = lane < 96, lane < 32, lane < 64
    odd = (lane // 32) % 2 == 1

    @pl.loop(0, RING)
    def _(p):
        last = [src[j, p, 8 * (3 * TILES + t) : 8 * (3 * TILES + t) + 8, :] for t in range(TILES - 2)]
        for t in (0, 3):
            r = [pltpu.roll(last[t + i], 32 * i + 32, 1) for i in range(3)]
            last.append(jnp.where(one, r[0], jnp.where(two, r[1], r[2])))
        for t in range(TILES):
            v = [src[j, p, 8 * (k * TILES + t) : 8 * (k * TILES + t) + 8, :] for k in range(3)]
            total = (v[0] + v[1]) + (v[2] + jnp.where(low, last[t], 0.0))
            total = jnp.where(odd, -total, total)
            total = total + pltpu.roll(total, 64, 1)
            total = total + pltpu.roll(total, 32, 1)
            v.append(jnp.where(low, last[t], total))
            for k in range(4):
                emit(p, 8 * t, k, v[k])


def smooth_z(src, dst, j):
    @pl.loop(0, SENT // 3)
    def _(t):
        for u in range(3):
            rows = tile(t * 24 + 8 * u)
            v = [src[j, q, rows, :] for q in range(RING + 4)]
            for _ in range(4):
                v = [v[q] + v[q + 1] for q in range(len(v) - 1)]
            for q in range(RING):
                dst[j, q, rows, :] = v[q] * SCALE


def kernel(x_ref, detail, coarse, xin, xs, ys, column, gathered, smoothed, back, early, before, after,
           load_sem, f_send, f_recv, b_send, b_recv, h_send, h_recv, x_send, x_recv):
    me = ring_index(0)
    hops = range(len(HOPS))

    def load(j):
        return pltpu.make_async_copy(x_ref.at[j], xin.at[j], load_sem.at[j])

    def forth(j, k):
        dy = HOPS[k]
        return pltpu.make_async_remote_copy(
            ys.at[j, ring_index(dy)], gathered.at[j, me + 2], f_send.at[j, k], f_recv.at[j, k],
            device_id=device(0, dy), device_id_type=MESH)

    def home(j, k):
        dy = HOPS[k]
        return pltpu.make_async_remote_copy(
            smoothed.at[j, ring_index(dy)], back.at[j, me], b_send.at[j, k], b_recv.at[j, k],
            device_id=device(0, dy), device_id_type=MESH)

    def halo(j, src, side):
        if side == 0:
            return pltpu.make_async_remote_copy(
                src.at[j, pl.ds(ROWS - HALO, HALO)], before.at[j], h_send.at[j, 0], h_recv.at[j, 0],
                device_id=gy_device(1), device_id_type=MESH)
        return pltpu.make_async_remote_copy(
            src.at[j, pl.ds(0, HALO)], after.at[j], h_send.at[j, 1], h_recv.at[j, 1],
            device_id=gy_device(3), device_id_type=MESH)

    def emit_packed(j, block, row, k, value):
        if k < 3:
            ys[j, block // 2, tile(PIECE * k + 32 * (block % 2) + row), :] = value
        else:
            column[tile(32 * block + row), :] = value

    def send_forth(j):
        pack_last(column, ys, j)
        for k in hops:
            forth(j, k).start()
        gathered[j, me + 2] = ys[j, me]

    def across(j, side):
        src, dst, dx = ((4, 0, 1), (2, 6, 3))[side]
        return pltpu.make_async_remote_copy(
            gathered.at[j, pl.ds(src, 2)], gathered.at[j, pl.ds(dst, 2)], x_send.at[j, side], x_recv.at[j, side],
            device_id=device(dx, 0), device_id_type=MESH)

    def step_x(j):
        for k in hops:
            forth(j, k).wait_recv()
        for side in range(2):
            across(j, side).start()

    def step_z(j):
        for side in range(2):
            across(j, side).wait_recv()
        smooth_z(gathered, smoothed, j)
        for k in hops:
            home(j, k).start()
        back[j, me] = smoothed[j, me]

    def step_y(j):
        for side in range(2):
            halo(j, xs, side).wait_recv()
        smooth_y(xs, before, after, j, lambda block, row, k, value: emit_packed(j, block, row, k, value))
        send_forth(j)

    def early_halo(j):
        for k in hops:
            home(j, k).wait_recv()

        def emit(p, row, k, value):
            early[j, tile(PIECE * p + row), 128 * k : 128 * k + 128] = value

        unpack(back, j, emit)
        for side in range(2):
            halo(j, early, side).start()

    def emit_out(j, start, k, value):
        rows, cols = tile(start), slice(128 * k, 128 * k + 128)
        coarse[j, rows, cols] = value
        detail[j, rows, cols] = xin[j, rows, cols] - value

    def early_finish(j):
        for side in range(2):
            halo(j, early, side).wait_recv()
        smooth_y(early, before, after, j, lambda block, row, k, value: emit_out(j, 32 * block + row, k, value))

    def late_finish(j):
        for k in hops:
            home(j, k).wait_recv()
        unpack(back, j, lambda p, row, k, value: emit_out(j, PIECE * p + row, k, value))

    def early_start(j):
        smooth_x(xin, j, lambda block, row, k, value: emit_packed(j, block, row, k, value))

    def late_start(j):
        def emit(block, row, k, value):
            xs[j, tile(32 * block + row), 128 * k : 128 * k + 128] = value

        smooth_x(xin, j, emit)
        for side in range(2):
            halo(j, xs, side).start()

    for j in range(PLANES):
        load(j).start()
    barrier = pltpu.get_barrier_semaphore()
    for dx, dy in GREET:
        pl.semaphore_signal(barrier, inc=1, device_id=device(dx, dy), device_id_type=MESH)
    for dh in (1, 3):
        pl.semaphore_signal(barrier, inc=1, device_id=gy_device(dh), device_id_type=MESH)
    load(0).wait()
    early_start(0)
    pl.semaphore_wait(barrier, len(GREET) + 2)
    send_forth(0)

    @pl.loop(1, EARLY)
    def _(j):
        load(j).wait()
        early_start(j)
        send_forth(j)

    @pl.loop(EARLY, PLANES)
    def _(j):
        load(j).wait()
        late_start(j)

    @pl.loop(0, PLANES + LAG2)
    def _(i):
        @pl.when(i < PLANES - EARLY)
        def _():
            step_y(i + EARLY)

        @pl.when(i < PLANES)
        def _():
            step_x(i)

        @pl.when((i >= LAGZ) & (i < LAGZ + PLANES))
        def _():
            step_z(i - LAGZ)

        @pl.when((i >= LAG1) & (i < LAG1 + EARLY))
        def _():
            early_halo(i - LAG1)

        @pl.when((i >= LAG2) & (i < LAG2 + EARLY))
        def _():
            early_finish(i - LAG2)

        @pl.when(i >= LAG2 + EARLY)
        def _():
            late_finish(i - LAG2)

    @pl.loop(0, PLANES)
    def _(j):
        for side in range(2):
            halo(j, xs, side).wait_send()
            across(j, side).wait_send()
        for k in hops:
            forth(j, k).wait_send()
            home(j, k).wait_send()


def shards(coarse_six):
    full = pltpu.VMEM((PLANES, ROWS, COLS), F32)

    def packed(n):
        return pltpu.VMEM((PLANES, n, 8 * SENT, 128), F32)

    edge = pltpu.VMEM((PLANES, HALO, COLS), F32)
    dma = pltpu.SemaphoreType.DMA
    n = len(HOPS)
    return pl.pallas_call(
        kernel,
        out_shape=(full, full),
        in_specs=[pl.BlockSpec(memory_space=pl.ANY)],
        out_specs=(pl.BlockSpec(memory_space=pltpu.VMEM),) * 2,
        scratch_shapes=[full, full, packed(RING), pltpu.VMEM((ROWS, 128), F32), packed(RING + 4), packed(RING), packed(RING),
                        pltpu.VMEM((EARLY, ROWS, COLS), F32), edge, edge,
                        dma((PLANES,)), dma((PLANES, n)), dma((PLANES, n)), dma((PLANES, n)), dma((PLANES, n)),
                        dma((PLANES, 2)), dma((PLANES, 2)), dma((PLANES, 2)), dma((PLANES, 2))],
        compiler_params=pltpu.CompilerParams(collective_id=0, has_side_effects=True, vmem_limit_bytes=50 << 20),
        name="starlet",
    )(coarse_six)


def solution(mesh):
    return jax.shard_map(
        shards,
        mesh=mesh,
        in_specs=(P("gz", "gy", None),),
        out_specs=(P("gz", "gy", None), P("gz", "gy", None)),
        check_vma=False,
    )
```

time: 121 us -> 102 us (0.84)
  the two profiles are of different devices: /device:TPU:188 before, /device:TPU:64 now
where the time goes in v2:
time: 102 us; the launch traced here: 99.9 us
  Pallas kernels  95.2 us (93%)
  local copies, waits for them, and re-layouts  4.03 us (4%)
    pallas_call x1, Pallas kernels, shards(): pl.pallas_call(kernel, out_shape=(full, full), in_specs=[pl.BlockSpec(mem...  95.2 us
    unnamed x2, local copies, waits for them, and re-layouts  4.03 us

profile of v2, /device:TPU:64, one launch (start us, length us, event | category | flops | bytes accessed | tf_op | source)
XLA Modules:
  0.0 99.9 jit_solution(1617291370564237677)
XLA Ops:
  0.6 95.2 %starlet.1 = (f32[8,256,512]{2,1,0:T(8,128)S(1)}, f32[8,256,512]{2,1,0:T(8,128)S(1)}) custom-call(f32[8,256,512]{2,1,0:T(8,128)} %x_ref.1), custom_call_target="tpu_custom_call" | custom-call | tf_op jit(solution)/shard_map/starlet/pallas_call | solution.py:301
  95.8 2.0 %copy.5 = f32[8,256,512]{2,1,0:T(8,128)} copy(f32[8,256,512]{2,1,0:T(8,128)S(1)} %get-tuple-element.2) | data formatting | bytes 8388608
  97.9 2.0 %copy.6 = f32[8,256,512]{2,1,0:T(8,128)} copy(f32[8,256,512]{2,1,0:T(8,128)S(1)} %get-tuple-element.3) | data formatting | bytes 8388608

commit v3 on v2

--- a/solution.py
+++ b/solution.py
@@ -21,7 +21,6 @@
 LAGZ, LAG1, LAG2 = 1, 4, 6
 SCALE = 1.0 / 4096.0
 HOPS = (1, 3, 2)
-GREET = ((0, 1), (0, 2), (0, 3), (1, 0), (3, 0))
 
 
 def place():
@@ -47,11 +46,11 @@
     return pl.ds(pl.multiple_of(start, 8), 8)
 
 
-def smooth_x(src, j, emit):
+def smooth_x(src, j, emit, first=0, count=ROWS // 32):
     lane = lax.broadcasted_iota(jnp.int32, (8, 128), 1)
     left, low, high = lane < 64, lane < 96, lane >= 32
 
-    @pl.loop(0, ROWS // 32)
+    @pl.loop(first, first + count)
     def _(t):
         for u in range(4):
             v = [src[j, tile(t * 32 + 8 * u), 128 * k : 128 * k + 128] for k in range(4)]
@@ -83,35 +82,32 @@
                 emit(i, t * 8, k, v[i])
 
 
-def pack_last(column, dst, j):
+def pack_last(column, dst, j, p):
     low = lax.broadcasted_iota(jnp.int32, (8, 128), 1) < 96
-    for p in range(RING):
-        v = [column[PIECE * p + 8 * t : PIECE * p + 8 * t + 8, :] for t in range(TILES)]
-        for t in range(TILES - 2):
-            moved = pltpu.roll(v[TILES - 2 + t // 3], 96 - 32 * (t % 3), 1)
-            dst[j, p, 8 * (3 * TILES + t) : 8 * (3 * TILES + t) + 8, :] = jnp.where(low, v[t], moved)
-
-
-def unpack(src, j, emit):
+    v = [column[tile(PIECE * p + 8 * t), :] for t in range(TILES)]
+    for t in range(TILES - 2):
+        moved = pltpu.roll(v[TILES - 2 + t // 3], 96 - 32 * (t % 3), 1)
+        dst[j, p, 8 * (3 * TILES + t) : 8 * (3 * TILES + t) + 8, :] = jnp.where(low, v[t], moved)
+
+
+def unpack(src, j, p, emit):
     lane = lax.broadcasted_iota(jnp.int32, (8, 128), 1)
     low, one, two = lane < 96, lane < 32, lane < 64
     odd = (lane // 32) % 2 == 1
 
-    @pl.loop(0, RING)
-    def _(p):
-        last = [src[j, p, 8 * (3 * TILES + t) : 8 * (3 * TILES + t) + 8, :] for t in range(TILES - 2)]
-        for t in (0, 3):
-            r = [pltpu.roll(last[t + i], 32 * i + 32, 1) for i in range(3)]
-            last.append(jnp.where(one, r[0], jnp.where(two, r[1], r[2])))
-        for t in range(TILES):
-            v = [src[j, p, 8 * (k * TILES + t) : 8 * (k * TILES + t) + 8, :] for k in range(3)]
-            total = (v[0] + v[1]) + (v[2] + jnp.where(low, last[t], 0.0))
-            total = jnp.where(odd, -total, total)
-            total = total + pltpu.roll(total, 64, 1)
-            total = total + pltpu.roll(total, 32, 1)
-            v.append(jnp.where(low, last[t], total))
-            for k in range(4):
-                emit(p, 8 * t, k, v[k])
+    last = [src[j, p, 8 * (3 * TILES + t) : 8 * (3 * TILES + t) + 8, :] for t in range(TILES - 2)]
+    for t in (0, 3):
+        r = [pltpu.roll(last[t + i], 32 * i + 32, 1) for i in range(3)]
+        last.append(jnp.where(one, r[0], jnp.where(two, r[1], r[2])))
+    for t in range(TILES):
+        v = [src[j, p, 8 * (k * TILES + t) : 8 * (k * TILES + t) + 8, :] for k in range(3)]
+        total = (v[0] + v[1]) + (v[2] + jnp.where(low, last[t], 0.0))
+        total = jnp.where(odd, -total, total)
+        total = total + pltpu.roll(total, 64, 1)
+        total = total + pltpu.roll(total, 32, 1)
+        v.append(jnp.where(low, last[t], total))
+        for k in range(4):
+            emit(p, 8 * t, k, v[k])
 
 
 def smooth_z(src, dst, j):
@@ -127,12 +123,16 @@
 
 
 def kernel(x_ref, detail, coarse, xin, xs, ys, column, gathered, smoothed, back, early, before, after,
-           load_sem, f_send, f_recv, b_send, b_recv, h_send, h_recv, x_send, x_recv):
+           ring_sem, near_sem, load_sem, first_sem, f_send, f_recv, b_send, b_recv, h_send, h_recv, x_send, x_recv):
     me = ring_index(0)
     hops = range(len(HOPS))
 
     def load(j):
         return pltpu.make_async_copy(x_ref.at[j], xin.at[j], load_sem.at[j])
+
+    def load_first(dy):
+        rows = pl.ds(pl.multiple_of(PIECE * ring_index(dy), PIECE), PIECE)
+        return pltpu.make_async_copy(x_ref.at[0, rows], xin.at[0, rows], first_sem.at[dy])
 
     def forth(j, k):
         dy = HOPS[k]
@@ -162,9 +162,10 @@
             column[tile(32 * block + row), :] = value
 
     def send_forth(j):
-        pack_last(column, ys, j)
-        for k in hops:
+        for k in hops:
+            pack_last(column, ys, j, ring_index(HOPS[k]))
             forth(j, k).start()
+        pack_last(column, ys, j, me)
         gathered[j, me + 2] = ys[j, me]
 
     def across(j, side):
@@ -193,14 +194,17 @@
         smooth_y(xs, before, after, j, lambda block, row, k, value: emit_packed(j, block, row, k, value))
         send_forth(j)
 
+    def arrive(j, emit):
+        unpack(back, j, me, emit)
+        for k in hops:
+            home(j, k).wait_recv()
+            unpack(back, j, ring_index(-HOPS[k]), emit)
+
     def early_halo(j):
-        for k in hops:
-            home(j, k).wait_recv()
-
         def emit(p, row, k, value):
             early[j, tile(PIECE * p + row), 128 * k : 128 * k + 128] = value
 
-        unpack(back, j, emit)
+        arrive(j, emit)
         for side in range(2):
             halo(j, early, side).start()
 
@@ -212,12 +216,24 @@
     def early_finish(j):
         for side in range(2):
             halo(j, early, side).wait_recv()
+        sent(j)
         smooth_y(early, before, after, j, lambda block, row, k, value: emit_out(j, 32 * block + row, k, value))
 
+    def sent(j):
+        for side in range(2):
+            halo(j, xs, side).wait_send()
+            across(j, side).wait_send()
+        for k in hops:
+            forth(j, k).wait_send()
+
+        @pl.when(j > 0)
+        def _():
+            for k in hops:
+                home(j - 1, k).wait_send()
+
     def late_finish(j):
-        for k in hops:
-            home(j, k).wait_recv()
-        unpack(back, j, lambda p, row, k, value: emit_out(j, PIECE * p + row, k, value))
+        sent(j)
+        arrive(j, lambda p, row, k, value: emit_out(j, PIECE * p + row, k, value))
 
     def early_start(j):
         smooth_x(xin, j, lambda block, row, k, value: emit_packed(j, block, row, k, value))
@@ -227,20 +243,44 @@
             xs[j, tile(32 * block + row), 128 * k : 128 * k + 128] = value
 
         smooth_x(xin, j, emit)
-        for side in range(2):
-            halo(j, xs, side).start()
-
-    for j in range(PLANES):
+
+    for dy in HOPS + (0,):
+        load_first(dy).start()
+    y = place()[1]
+    barrier = pltpu.get_barrier_semaphore()
+    for dy in HOPS:
+        @pl.when((y + dy) % 4 != 0)
+        def _():
+            pl.semaphore_signal(barrier, inc=1, device_id=device(0, dy), device_id_type=MESH)
+
+    for j in range(1, PLANES):
         load(j).start()
-    barrier = pltpu.get_barrier_semaphore()
-    for dx, dy in GREET:
-        pl.semaphore_signal(barrier, inc=1, device_id=device(dx, dy), device_id_type=MESH)
-    for dh in (1, 3):
-        pl.semaphore_signal(barrier, inc=1, device_id=gy_device(dh), device_id_type=MESH)
-    load(0).wait()
-    early_start(0)
-    pl.semaphore_wait(barrier, len(GREET) + 2)
-    send_forth(0)
+
+    def first_piece(dy):
+        load_first(dy).wait()
+        p = ring_index(dy)
+        smooth_x(xin, 0, lambda block, row, k, value: emit_packed(0, block, row, k, value), 2 * p, 2)
+        pack_last(column, ys, 0, p)
+
+    first_piece(HOPS[0])
+
+    @pl.when(y != 0)
+    def _():
+        pl.semaphore_wait(barrier, 3)
+        pl.semaphore_signal(ring_sem, inc=1, device_id=device(0, 4 - y), device_id_type=MESH)
+
+    @pl.when(y == 0)
+    def _():
+        pl.semaphore_wait(ring_sem, 3)
+        for there in (device(1, 0), device(3, 0), gy_device(1), gy_device(3)):
+            pl.semaphore_signal(barrier, inc=1, device_id=there, device_id_type=MESH)
+
+    forth(0, 0).start()
+    for k in hops[1:]:
+        first_piece(HOPS[k])
+        forth(0, k).start()
+    first_piece(0)
+    gathered[0, me + 2] = ys[0, me]
 
     @pl.loop(1, EARLY)
     def _(j):
@@ -253,6 +293,21 @@
         load(j).wait()
         late_start(j)
 
+    @pl.when(y == 0)
+    def _():
+        pl.semaphore_wait(barrier, 4)
+        for dy in HOPS:
+            pl.semaphore_signal(near_sem, inc=1, device_id=device(0, dy), device_id_type=MESH)
+
+    @pl.when(y != 0)
+    def _():
+        pl.semaphore_wait(near_sem, 1)
+
+    @pl.loop(EARLY, PLANES)
+    def _(j):
+        for side in range(2):
+            halo(j, xs, side).start()
+
     @pl.loop(0, PLANES + LAG2)
     def _(i):
         @pl.when(i < PLANES - EARLY)
@@ -279,14 +334,8 @@
         def _():
             late_finish(i - LAG2)
 
-    @pl.loop(0, PLANES)
-    def _(j):
-        for side in range(2):
-            halo(j, xs, side).wait_send()
-            across(j, side).wait_send()
-        for k in hops:
-            forth(j, k).wait_send()
-            home(j, k).wait_send()
+    for k in hops:
+        home(PLANES - 1, k).wait_send()
 
 
 def shards(coarse_six):
@@ -305,7 +354,7 @@
         out_specs=(pl.BlockSpec(memory_space=pltpu.VMEM),) * 2,
         scratch_shapes=[full, full, packed(RING), pltpu.VMEM((ROWS, 128), F32), packed(RING + 4), packed(RING), packed(RING),
                         pltpu.VMEM((EARLY, ROWS, COLS), F32), edge, edge,
-                        dma((PLANES,)), dma((PLANES, n)), dma((PLANES, n)), dma((PLANES, n)), dma((PLANES, n)),
+                        pltpu.SemaphoreType.REGULAR, pltpu.SemaphoreType.REGULAR, dma((PLANES,)), dma((RING,)), dma((PLANES, n)), dma((PLANES, n)), dma((PLANES, n)), dma((PLANES, n)),
                         dma((PLANES, 2)), dma((PLANES, 2)), dma((PLANES, 2)), dma((PLANES, 2))],
         compiler_params=pltpu.CompilerParams(collective_id=0, has_side_effects=True, vmem_limit_bytes=50 << 20),
         name="starlet",

time: 102 us -> 106 us (1.039)
  the two profiles are of different devices: /device:TPU:64 before, /device:TPU:36 now
where the time goes in v3:
time: 106 us; the launch traced here: 105 us
  Pallas kernels  101 us (95%)
  local copies, waits for them, and re-layouts  4.03 us (4%)
    pallas_call x1, Pallas kernels, shards(): pl.pallas_call(kernel, out_shape=(full, full), in_specs=[pl.BlockSpec(mem...  101 us
    unnamed x2, local copies, waits for them, and re-layouts  4.03 us

profile of v3, /device:TPU:36, one launch (start us, length us, event | category | flops | bytes accessed | tf_op | source)
XLA Modules:
  0.0 105.4 jit_solution(6110480540472025879)
XLA Ops:
  0.6 100.8 %starlet.1 = (f32[8,256,512]{2,1,0:T(8,128)S(1)}, f32[8,256,512]{2,1,0:T(8,128)S(1)}) custom-call(f32[8,256,512]{2,1,0:T(8,128)} %x_ref.1), custom_call_target="tpu_custom_call" | custom-call | tf_op jit(solution)/shard_map/starlet/pallas_call | solution.py:350
  101.4 2.0 %copy.5 = f32[8,256,512]{2,1,0:T(8,128)} copy(f32[8,256,512]{2,1,0:T(8,128)S(1)} %get-tuple-element.2) | data formatting | bytes 8388608
  103.4 2.0 %copy.6 = f32[8,256,512]{2,1,0:T(8,128)} copy(f32[8,256,512]{2,1,0:T(8,128)S(1)} %get-tuple-element.3) | data formatting | bytes 8388608

commit v4 on v3

--- a/solution.py
+++ b/solution.py
@@ -17,8 +17,8 @@
 SENT = 3 * TILES + TILES - 2
 DIL = 32
 HALO = 2 * DIL
-EARLY = 4
-LAGZ, LAG1, LAG2 = 1, 4, 6
+EARLY = 5
+LAGY, LAGZ, LAG1, LAG2 = 1, 1, 4, 6
 SCALE = 1.0 / 4096.0
 HOPS = (1, 3, 2)
 
@@ -310,10 +310,6 @@
 
     @pl.loop(0, PLANES + LAG2)
     def _(i):
-        @pl.when(i < PLANES - EARLY)
-        def _():
-            step_y(i + EARLY)
-
         @pl.when(i < PLANES)
         def _():
             step_x(i)
@@ -321,6 +317,10 @@
         @pl.when((i >= LAGZ) & (i < LAGZ + PLANES))
         def _():
             step_z(i - LAGZ)
+
+        @pl.when((i >= LAGY) & (i < LAGY + PLANES - EARLY))
+        def _():
+            step_y(i + EARLY - LAGY)
 
         @pl.when((i >= LAG1) & (i < LAG1 + EARLY))
         def _():

time: 106 us -> 96.7 us (0.912)
  the two profiles are of different devices: /device:TPU:36 before, /device:TPU:64 now
where the time goes in v4:
time: 96.7 us; the launch traced here: 96 us
  Pallas kernels  91.3 us (94%)
  local copies, waits for them, and re-layouts  4.03 us (4%)
    pallas_call x1, Pallas kernels, shards(): pl.pallas_call(kernel, out_shape=(full, full), in_specs=[pl.BlockSpec(mem...  91.3 us
    unnamed x2, local copies, waits for them, and re-layouts  4.03 us

profile of v4, /device:TPU:64, one launch (start us, length us, event | category | flops | bytes accessed | tf_op | source)
XLA Modules:
  0.0 96.0 jit_solution(13229542806675189388)
XLA Ops:
  0.6 91.3 %starlet.1 = (f32[8,256,512]{2,1,0:T(8,128)S(1)}, f32[8,256,512]{2,1,0:T(8,128)S(1)}) custom-call(f32[8,256,512]{2,1,0:T(8,128)} %x_ref.1), custom_call_target="tpu_custom_call" | custom-call | tf_op jit(solution)/shard_map/starlet/pallas_call | solution.py:350
  91.9 2.0 %copy.5 = f32[8,256,512]{2,1,0:T(8,128)} copy(f32[8,256,512]{2,1,0:T(8,128)S(1)} %get-tuple-element.2) | data formatting | bytes 8388608
  94.0 2.0 %copy.6 = f32[8,256,512]{2,1,0:T(8,128)} copy(f32[8,256,512]{2,1,0:T(8,128)S(1)} %get-tuple-element.3) | data formatting | bytes 8388608

commit v5 on v4

--- a/solution.py
+++ b/solution.py
@@ -338,6 +338,15 @@
         home(PLANES - 1, k).wait_send()
 
 
+def write_out(detail, coarse, detail_ref, coarse_ref, sem):
+    copies = [pltpu.make_async_copy(src.at[j], dst.at[j], sem.at[i, j])
+              for j in range(PLANES) for i, (src, dst) in enumerate(((detail, detail_ref), (coarse, coarse_ref)))]
+    for copy in copies:
+        copy.start()
+    for copy in copies:
+        copy.wait()
+
+
 def shards(coarse_six):
     full = pltpu.VMEM((PLANES, ROWS, COLS), F32)
 
@@ -347,7 +356,7 @@
     edge = pltpu.VMEM((PLANES, HALO, COLS), F32)
     dma = pltpu.SemaphoreType.DMA
     n = len(HOPS)
-    return pl.pallas_call(
+    results = pl.pallas_call(
         kernel,
         out_shape=(full, full),
         in_specs=[pl.BlockSpec(memory_space=pl.ANY)],
@@ -359,6 +368,16 @@
         compiler_params=pltpu.CompilerParams(collective_id=0, has_side_effects=True, vmem_limit_bytes=50 << 20),
         name="starlet",
     )(coarse_six)
+    block = jax.ShapeDtypeStruct((PLANES, ROWS, COLS), F32)
+    return pl.pallas_call(
+        write_out,
+        out_shape=(block, block),
+        in_specs=[pl.BlockSpec(memory_space=pl.ANY)] * 2,
+        out_specs=(pl.BlockSpec(memory_space=pl.ANY),) * 2,
+        scratch_shapes=[dma((2, PLANES))],
+        compiler_params=pltpu.CompilerParams(vmem_limit_bytes=1 << 20),
+        name="write_out",
+    )(*results)
 
 
 def solution(mesh):

time: 96.7 us -> 96.1 us (level)
  local copies, waits for them, and re-layouts: 4.03 us -> 0 us
  Pallas kernels: 91.3 us -> 94.7 us
    unnamed x2 -> x0, local copies, waits for them, and re-layouts: 4.03 us -> none
    pallas_call x0 -> x1, Pallas kernels: none -> 3.42 us  [shards(): pl.pallas_call(write_out, out_shape=(block, block), in_specs=[pl.BlockSpe...]
where the time goes in v5:
time: 96.1 us; the launch traced here: 95.4 us
  Pallas kernels  94.7 us (99%)
    pallas_call x1, Pallas kernels, shards(): pl.pallas_call(kernel, out_shape=(full, full), in_specs=[pl.BlockSpec(mem...  91.3 us
    pallas_call x1, Pallas kernels, shards(): pl.pallas_call(write_out, out_shape=(block, block), in_specs=[pl.BlockSpe...  3.42 us

profile of v5, /device:TPU:64, one launch (start us, length us, event | category | flops | bytes accessed | tf_op | source)
XLA Modules:
  0.0 95.4 jit_solution(15236809500523393618)
XLA Ops:
  0.6 91.3 %starlet.1 = (f32[8,256,512]{2,1,0:T(8,128)S(1)}, f32[8,256,512]{2,1,0:T(8,128)S(1)}) custom-call(f32[8,256,512]{2,1,0:T(8,128)} %x_ref.1), custom_call_target="tpu_custom_call" | custom-call | tf_op jit(solution)/shard_map/starlet/pallas_call | solution.py:359
  91.9 3.4 %write_out.1 = (f32[8,256,512]{2,1,0:T(8,128)}, f32[8,256,512]{2,1,0:T(8,128)}) custom-call(f32[8,256,512]{2,1,0:T(8,128)S(1)} %get-tuple-element.4.detail, f32[8,256,512]{2,1,0:T(8,128)S(1)} %get-tuple-element.5.coarse), custom_call_target="tpu_custom_call" | custom-call | tf_op jit(solution)/shard_map/write_out/pallas_call | solution.py:372

commit v6 on v5

--- a/solution.py
+++ b/solution.py
@@ -122,7 +122,7 @@
                 dst[j, q, rows, :] = v[q] * SCALE
 
 
-def kernel(x_ref, detail, coarse, xin, xs, ys, column, gathered, smoothed, back, early, before, after,
+def kernel(x_ref, detail, coarse, xin, back, xs, ys, column, gathered, smoothed, early, before, after,
            ring_sem, near_sem, load_sem, first_sem, f_send, f_recv, b_send, b_recv, h_send, h_recv, x_send, x_recv):
     me = ring_index(0)
     hops = range(len(HOPS))
@@ -233,7 +233,15 @@
 
     def late_finish(j):
         sent(j)
-        arrive(j, lambda p, row, k, value: emit_out(j, PIECE * p + row, k, value))
+
+        @pl.when(j < PLANES - 1)
+        def _():
+            arrive(j, lambda p, row, k, value: emit_out(j, PIECE * p + row, k, value))
+
+        @pl.when(j == PLANES - 1)
+        def _():
+            for k in hops:
+                home(j, k).wait_recv()
 
     def early_start(j):
         smooth_x(xin, j, lambda block, row, k, value: emit_packed(j, block, row, k, value))
@@ -338,12 +346,27 @@
         home(PLANES - 1, k).wait_send()
 
 
-def write_out(detail, coarse, detail_ref, coarse_ref, sem):
+def write_out(detail, coarse, xin, back, detail_ref, coarse_ref, last_detail, last_coarse, sem):
+    last = PLANES - 1
     copies = [pltpu.make_async_copy(src.at[j], dst.at[j], sem.at[i, j])
-              for j in range(PLANES) for i, (src, dst) in enumerate(((detail, detail_ref), (coarse, coarse_ref)))]
+              for j in range(last) for i, (src, dst) in enumerate(((detail, detail_ref), (coarse, coarse_ref)))]
     for copy in copies:
         copy.start()
-    for copy in copies:
+
+    def emit(p, row, k, value):
+        rows, cols = tile(PIECE * p + row), slice(128 * k, 128 * k + 128)
+        last_coarse[rows, cols] = value
+        last_detail[rows, cols] = xin[last, rows, cols] - value
+
+    @pl.loop(0, RING)
+    def _(p):
+        unpack(back, last, p, emit)
+
+    ends = [pltpu.make_async_copy(src, dst.at[last], sem.at[i, last])
+            for i, (src, dst) in enumerate(((last_detail, detail_ref), (last_coarse, coarse_ref)))]
+    for copy in ends:
+        copy.start()
+    for copy in copies + ends:
         copy.wait()
 
 
@@ -358,24 +381,24 @@
     n = len(HOPS)
     results = pl.pallas_call(
         kernel,
-        out_shape=(full, full),
+        out_shape=(full, full, full, packed(RING)),
         in_specs=[pl.BlockSpec(memory_space=pl.ANY)],
-        out_specs=(pl.BlockSpec(memory_space=pltpu.VMEM),) * 2,
-        scratch_shapes=[full, full, packed(RING), pltpu.VMEM((ROWS, 128), F32), packed(RING + 4), packed(RING), packed(RING),
+        out_specs=(pl.BlockSpec(memory_space=pltpu.VMEM),) * 4,
+        scratch_shapes=[full, packed(RING), pltpu.VMEM((ROWS, 128), F32), packed(RING + 4), packed(RING),
                         pltpu.VMEM((EARLY, ROWS, COLS), F32), edge, edge,
                         pltpu.SemaphoreType.REGULAR, pltpu.SemaphoreType.REGULAR, dma((PLANES,)), dma((RING,)), dma((PLANES, n)), dma((PLANES, n)), dma((PLANES, n)), dma((PLANES, n)),
                         dma((PLANES, 2)), dma((PLANES, 2)), dma((PLANES, 2)), dma((PLANES, 2))],
-        compiler_params=pltpu.CompilerParams(collective_id=0, has_side_effects=True, vmem_limit_bytes=50 << 20),
+        compiler_params=pltpu.CompilerParams(collective_id=0, has_side_effects=True, vmem_limit_bytes=42 << 20),
         name="starlet",
     )(coarse_six)
     block = jax.ShapeDtypeStruct((PLANES, ROWS, COLS), F32)
     return pl.pallas_call(
         write_out,
         out_shape=(block, block),
-        in_specs=[pl.BlockSpec(memory_space=pl.ANY)] * 2,
+        in_specs=[pl.BlockSpec(memory_space=pl.ANY)] * 2 + [pl.BlockSpec(memory_space=pltpu.VMEM)] * 2,
         out_specs=(pl.BlockSpec(memory_space=pl.ANY),) * 2,
-        scratch_shapes=[dma((2, PLANES))],
-        compiler_params=pltpu.CompilerParams(vmem_limit_bytes=1 << 20),
+        scratch_shapes=[pltpu.VMEM((ROWS, COLS), F32), pltpu.VMEM((ROWS, COLS), F32), dma((2, PLANES))],
+        compiler_params=pltpu.CompilerParams(vmem_limit_bytes=16 << 20),
         name="write_out",
     )(*results)
 

time: 96.1 us -> 95.9 us (level)
  no operation moved by 1% of the time
where the time goes in v6:
time: 95.9 us; the launch traced here: 95.1 us
  Pallas kernels  94.5 us (99%)
    pallas_call x1, Pallas kernels, shards(): pl.pallas_call(kernel, out_shape=(full, full, full, packed(RING)), in_spe...  91.1 us
    pallas_call x1, Pallas kernels, shards(): pl.pallas_call(write_out, out_shape=(block, block), in_specs=[pl.BlockSpe...  3.42 us

profile of v6, /device:TPU:64, one launch (start us, length us, event | category | flops | bytes accessed | tf_op | source)
XLA Modules:
  0.0 95.1 jit_solution(4651308452606537400)
XLA Ops:
  0.6 91.1 %starlet.1 = (f32[8,256,512]{2,1,0:T(8,128)S(1)}, f32[8,256,512]{2,1,0:T(8,128)S(1)}, f32[8,256,512]{2,1,0:T(8,128)S(1)}, f32[8,4,240,128]{3,2,1,0:T(8,128)S(1)}) custom-call(f32[8,256,512]{2,1,0:T(8,128)} %x_ref.1), custom_call_target="tpu_custom_call" | custom-call | tf_op jit(solution)/shard_map/starlet/pallas_call | solution.py:382
  91.7 3.4 %write_out.1 = (f32[8,256,512]{2,1,0:T(8,128)}, f32[8,256,512]{2,1,0:T(8,128)}) custom-call(f32[8,256,512]{2,1,0:T(8,128)S(1)} %get-tuple-element.6.detail, f32[8,256,512]{2,1,0:T(8,128)S(1)} %get-tuple-element.7.coarse, f32[8,256,512]{2,1,0:T(8,128)S(1)} %get-tuple-element.8.xin, f32[8,4,240,128]{3,2,1,0:T(8,128)S(1)} %get-tuple-element.9.back), custom_call_target="tpu_custom_call" | custom-call | tf_op jit(solution)/shard_map/write_out/pallas_call | solution.py:395

commit v7 on v6

--- a/solution.py
+++ b/solution.py
@@ -18,7 +18,7 @@
 DIL = 32
 HALO = 2 * DIL
 EARLY = 5
-LAGY, LAGZ, LAG1, LAG2 = 1, 1, 4, 6
+LAGY, LAGZ, LAG1, LAG2 = 1, 1, 3, 5
 SCALE = 1.0 / 4096.0
 HOPS = (1, 3, 2)
 

time: 95.9 us -> 95.9 us (level)
  no operation moved by 1% of the time
where the time goes in v7:
time: 95.9 us; the launch traced here: 95.1 us
  Pallas kernels  94.5 us (99%)
    pallas_call x1, Pallas kernels, shards(): pl.pallas_call(kernel, out_shape=(full, full, full, packed(RING)), in_spe...  91.1 us
    pallas_call x1, Pallas kernels, shards(): pl.pallas_call(write_out, out_shape=(block, block), in_specs=[pl.BlockSpe...  3.42 us

profile of v7, /device:TPU:64, one launch (start us, length us, event | category | flops | bytes accessed | tf_op | source)
XLA Modules:
  0.0 95.1 jit_solution(1755732671337967870)
XLA Ops:
  0.6 91.1 %starlet.1 = (f32[8,256,512]{2,1,0:T(8,128)S(1)}, f32[8,256,512]{2,1,0:T(8,128)S(1)}, f32[8,256,512]{2,1,0:T(8,128)S(1)}, f32[8,4,240,128]{3,2,1,0:T(8,128)S(1)}) custom-call(f32[8,256,512]{2,1,0:T(8,128)} %x_ref.1), custom_call_target="tpu_custom_call" | custom-call | tf_op jit(solution)/shard_map/starlet/pallas_call | solution.py:382
  91.7 3.4 %write_out.1 = (f32[8,256,512]{2,1,0:T(8,128)}, f32[8,256,512]{2,1,0:T(8,128)}) custom-call(f32[8,256,512]{2,1,0:T(8,128)S(1)} %get-tuple-element.6.detail, f32[8,256,512]{2,1,0:T(8,128)S(1)} %get-tuple-element.7.coarse, f32[8,256,512]{2,1,0:T(8,128)S(1)} %get-tuple-element.8.xin, f32[8,4,240,128]{3,2,1,0:T(8,128)S(1)} %get-tuple-element.9.back), custom_call_target="tpu_custom_call" | custom-call | tf_op jit(solution)/shard_map/write_out/pallas_call | solution.py:395
